TPU v7x, 32 devices: a whole 2x2x4 slice. The times are simulated.
32 devices in a mesh: dp: 4 (over x, core), expert: 2 (over y), etp: 4 (over z).
Axes of the slice: x: 2, y: 2, z: 4, core: 2. Of those that a mesh axis runs over, the one named last changes fastest.
Arguments:
- tokens: bfloat16 [1024, 6144], P(('dp', 'expert'), 'etp'), may hold values from -6 to 6
- routes: int32 [1024, 2], P(('dp', 'expert')), may hold values from 0 to 1, as said below
- gate_scale: float32 [1024, 2], P(('dp', 'expert')), may hold values from 0.2 to 1
- gate_weight: bfloat16 [2, 128, 6, 128, 128], P('expert', 'etp'), may hold values from -0.21875 to 0.21875
- up_weight: bfloat16 [2, 128, 6, 128, 128], P('expert', 'etp'), may hold values from -0.21875 to 0.21875
- down_weight: bfloat16 [2, 16, 48, 128, 128], P('expert', 'etp'), may hold values from -0.125 to 0.125
- gate_blocks: int32 [2, 128, 6], P('expert', 'etp'), may hold values from 0 to 47, as said below
- down_blocks: int32 [2, 16, 48], P('expert', 'etp'), may hold values from 0 to 7
Outputs:
- mixed: bfloat16 [1024, 6144], P(('dp', 'expert'), 'etp')
Inputs may be any that keep to these rules, and one draw needn't show every extreme that they name: `routes`: the two entries of a token name different experts. In each aligned block of 128 rows no expert is named more than 128 times, and one expert, the same for all blocks, is named exactly 128 times in every block. `gate_blocks`: for each expert and hidden block the 6 entries are different.
All inputs are finite; a program needn't handle non-finite values.
Results may differ from a plain program's by a relative error of at most 0.011.
Values may be sent and summed in bfloat16 or wider, within the bound.
No kernel may reach another device: no remote copies, remote signals or barrier semaphores. Data moves between devices by JAX's collectives and lax.ppermute only.
A program may use at most 128 MiB of HBM per device.

v0:
```python
import jax
import jax.numpy as jnp
from jax import lax
from jax.sharding import PartitionSpec as P


def slot_places(route_rows, expert_count, capacity):
    flat_routes = route_rows.reshape(-1)
    onehot = (flat_routes[:, None] == jnp.arange(expert_count, dtype=jnp.int32)[None, :]).astype(
        jnp.int32
    )
    earlier = jnp.cumsum(onehot, axis=0) - onehot
    slot_place = jnp.sum(earlier * onehot, axis=1)
    return flat_routes * capacity + slot_place


def expert_layer(token_rows, gate_part, up_part, down_part, gate_pick, down_pick):
    row_count = token_rows.shape[0]
    model_width = token_rows.shape[1]
    block_size = gate_part.shape[-1]
    hidden_count = gate_part.shape[0]
    keep_count = gate_part.shape[1]
    group_count = down_part.shape[0]
    group_size = hidden_count // group_count
    tiles = token_rows.reshape(row_count, model_width // block_size, block_size)
    picked = jnp.take(tiles, gate_pick.reshape(-1), axis=1).reshape(
        row_count, hidden_count, keep_count, block_size
    )
    gate_act = jnp.einsum("rfki,fkio->rfo", picked, gate_part, preferred_element_type=jnp.float32)
    up_act = jnp.einsum("rfki,fkio->rfo", picked, up_part, preferred_element_type=jnp.float32)
    hidden = (jax.nn.silu(gate_act) * up_act).astype(jnp.bfloat16)
    sources = down_pick + (jnp.arange(group_count, dtype=jnp.int32) * group_size)[:, None]
    chosen = jnp.take(hidden, sources.reshape(-1), axis=1).reshape(
        row_count, group_count, model_width // block_size, block_size
    )
    partial_value = jnp.einsum(
        "rgbi,gbio->rbo", chosen, down_part, preferred_element_type=jnp.float32
    )
    return partial_value.reshape(row_count, model_width)


def body(tokens, routes, gate_scale, gate_weight, up_weight, down_weight, gate_blocks, down_blocks):
    tok_count = tokens.shape[0]
    local_width = tokens.shape[1]
    group_total = lax.axis_size("expert")
    capacity = min(tok_count, 5 * tok_count // (2 * group_total))
    destination = slot_places(routes, group_total, capacity)
    filler = jnp.full((group_total * capacity,), tok_count, jnp.int32)
    anchor = filler.at[destination].set(jnp.arange(2 * tok_count, dtype=jnp.int32) // 2)
    outgoing = jnp.take(tokens, anchor, axis=0, mode="fill", fill_value=0)
    outgoing = outgoing.reshape(group_total, capacity, local_width)
    incoming = lax.all_to_all(outgoing, "expert", split_axis=0, concat_axis=0, tiled=True)
    arrived = lax.all_gather(incoming, "etp", axis=2, tiled=True)
    full_width = arrived.shape[2]
    partial_value = expert_layer(
        arrived.reshape(group_total * capacity, full_width),
        gate_weight[0],
        up_weight[0],
        down_weight[0],
        gate_blocks[0],
        down_blocks[0],
    )
    partial_value = partial_value.reshape(group_total, capacity, full_width)
    summed = lax.psum_scatter(
        partial_value.astype(jnp.bfloat16), "etp", scatter_dimension=2, tiled=True
    )
    returned = lax.all_to_all(summed, "expert", split_axis=0, concat_axis=0, tiled=True)
    returned = returned.reshape(group_total * capacity, local_width)
    fetched = (
        jnp.take(returned, destination, axis=0)
        .reshape(tok_count, 2, local_width)
        .astype(jnp.float32)
    )
    mixed = jnp.sum(fetched * gate_scale[:, :, None], axis=1)
    return mixed.astype(jnp.bfloat16)


def solution(mesh):
    placed = (
        P(("dp", "expert"), "etp"),
        P(("dp", "expert"), None),
        P(("dp", "expert"), None),
        P("expert", "etp", None, None, None),
        P("expert", "etp", None, None, None),
        P("expert", "etp", None, None, None),
        P("expert", "etp", None),
        P("expert", "etp", None),
    )
    return jax.shard_map(
        body, mesh=mesh, in_specs=placed, out_specs=P(("dp", "expert"), "etp"), check_vma=False
    )
```

profile of v0, /device:TPU:0, one launch (start us, length us, event | category | flops | bytes accessed | tf_op | source)
XLA Modules:
  0.0 239.1 jit_solution(16709429015321153645)
XLA Ops:
  6.5 0.8 copy.36
  7.4 0.1 eq.26
  7.5 0.1 reshape.162
  7.7 0.7 broadcast_multiply_fusion
  8.4 0.6 reduce-window.6
  9.0 0.2 slice_reduce_fusion
  9.2 0.2 reduce-window.9
  9.4 0.1 add_bitcast_fusion
  9.4 0.1 copy.42
  9.6 0.1 mul.46
  9.7 1.4 scatter_custom_fusion
  11.2 1.3 gather_fusion
  12.5 0.1 broadcast_select_fusion.6
  12.6 15.5 %all_to_all.10 = bf16[2,128,1536]{2,1,0:T(8,128)(2,1)} all-to-all(bf16[2,128,1536]{2,1,0:T(8,128)(2,1)S(1)} %broadcast_select_fusion.6), channel_id=1, replica_groups=mesh['dp'=4,'expert'=2,'etp'=4] {'expert'}, dimensions={0} | all-to-all | bytes 1572864 | tf_op jit(solution)/shard_map/all_to_all | solution.py:52
  28.1 0.0 all-gather.2.cloned.1.call-update
  28.1 0.2 reduce-scatter.2.cloned.1.call-start
  28.3 0.1 copy.43
  28.4 0.1 reshape_squeeze.6
  28.6 0.1 copy.41
  28.7 0.1 add.124
  28.7 0.1 add.137
  28.8 0.1 squeeze.17
  28.9 0.1 compare_and_fusion.1
  29.0 0.1 copy.40
  29.1 63.1 %all-gather.2.cloned.1.call-done = bf16[2,128,6144]{2,1,0:T(8,128)(2,1)} async-done(((bf16[2,128,1536]{2,1,0:T(8,128)(2,1)}), bf16[2,128,6144]{2,1,0:T(8,128)(2,1)}) %all-gather.2.cloned.1.call-update) | async-done | bytes 3145744 | tf_op jit(solution)/shard_map/all_gather | solution.py:53
  92.2 2.6 %copy.54 = bf16[32,8,48,128]{3,2,1,0:T(8,128)(2,1)S(1)} copy(bf16[32,8,48,128]{3,1,2,0:T(8,128)(2,1)} %bitcast.93) | data formatting | bytes 6291456
  94.8 0.8 copy.44
  95.7 8.2 %gather_fusion.1 = bf16[192,256,128]{2,1,0:T(8,128)(2,1)} fusion(bf16[256,48,128]{2,0,1:T(8,128)(2,1)S(1)} %copy.44, s32[1024]{0:T(1024)S(1)} %pad_clamp_fusion.2), kind=kCustom, calls=%fused_computation.1 | custom fusion | bytes 25166592 | tf_op jit(solution)/shard_map/jit(_take)/gather | solution.py:26
  103.9 11.8 %fusion.3 = f32[32,256,128,1]{2,1,3,0:T(8,128)} fusion(bf16[256,32,6,128]{3,0,2,1:T(8,128)(2,1)} %bitcast.89, pred[32,6]{1,0:T(8,128)(4,1)S(1)} %copy.41, bf16[1,32,6,128,128]{4,3,2,1,0:T(8,128)(2,1)} %param.11), kind=kOutput, calls=%fused_computation.10 | convolution fusion | flops 1616904192 | bytes 23068864 | tf_op jit(solution)/shard_map/rfki,fkio->rfo/dot_general | solution.py:29
  115.7 11.1 %fusion.10 = bf16[256,32,128]{2,0,1:T(8,128)(2,1)S(1)} fusion(f32[32,256,128,1]{2,1,3,0:T(8,128)} %fusion.3, bf16[1,32,6,128,128]{4,3,2,1,0:T(8,128)(2,1)} %param.12, bf16[256,32,6,128]{3,0,2,1:T(8,128)(2,1)} %bitcast.90, pred[32,6]{1,0:T(8,128)(4,1)S(1)} %copy.41), kind=kOutput, calls=%fused_computation.19 | convolution fusion | flops 1623195648 | bytes 25166016 | tf_op jit(solution)/shard_map/rfki,fkio->rfo/dot_general | solution.py:30
  126.8 8.2 %gather_fusion.2 = bf16[192,256,128]{2,1,0:T(8,128)(2,1)} fusion(bf16[256,32,128]{2,0,1:T(8,128)(2,1)S(1)} %fusion.10, s32[1024]{0:T(1024)S(1)} %pad_clamp_fusion.1), kind=kCustom, calls=%fused_computation.2 | custom fusion | bytes 25166592 | tf_op jit(solution)/shard_map/jit(_take)/gather | solution.py:33
  135.1 11.5 %fusion.14 = bf16[256,48,128]{2,0,1:T(8,128)(2,1)} fusion(bf16[256,4,48,128]{3,0,2,1:T(8,128)(2,1)} %bitcast.91, pred[4,48]{0,1:T(8,128)(4,1)S(1)} %copy.40, bf16[1,4,48,128,128]{4,3,2,1,0:T(8,128)(2,1)} %param.13), kind=kOutput, calls=%fused_computation.25 | convolution fusion | flops 1618477056 | bytes 22020288 | tf_op jit(solution)/shard_map/rgbi,gbio->rbo/dot_general | solution.py:36
  146.6 3.9 %copy.47 = bf16[256,48,128]{2,1,0:T(8,128)(2,1)S(1)} copy(bf16[256,48,128]{2,0,1:T(8,128)(2,1)} %fusion.14) | data formatting | bytes 6291456 | tf_op jit(solution)/shard_map/convert_element_type | solution.py:65
  150.5 0.0 copy-start.3
  150.5 0.0 copy-start.5
  150.5 2.8 %convert_element_type.30 = bf16[2,128,6144]{2,1,0:T(8,128)(2,1)} reshape(bf16[256,48,128]{2,1,0:T(8,128)(2,1)S(1)} %copy.47) | data formatting | bytes 6291456 | tf_op jit(solution)/shard_map/convert_element_type | solution.py:65
  153.4 0.0 reduce-scatter.2.cloned.1.call-update
  153.4 0.0 copy-start.1
  153.4 59.2 %reduce-scatter.2.cloned.1.call-done = bf16[2,128,1536]{2,1,0:T(8,128)(2,1)} async-done(((bf16[2,128,6144]{2,1,0:T(8,128)(2,1)}), bf16[2,128,1536]{2,1,0:T(8,128)(2,1)}) %reduce-scatter.2.cloned.1.call-update) | async-done | bytes 786448 | tf_op jit(solution)/shard_map/reduce_scatter | solution.py:64
  212.6 3.5 %all-to-all-start.1 = ((bf16[2,128,1536]{2,1,0:T(8,128)(2,1)}), bf16[2,128,1536]{2,1,0:T(8,128)(2,1)S(1)}, u32[]{:S(2)}, u32[]{:S(2)}) async-start(bf16[2,128,1536]{2,1,0:T(8,128)(2,1)} %reduce-scatter.2.cloned.1.call-done), calls=%async_computation.2 | async-start | bytes 1572864 | tf_op jit(solution)/shard_map/all_to_all | solution.py:67
  216.1 0.1 reduce_sum.23
  216.3 0.1 copy.38
  216.4 0.1 copy.39
  216.5 0.1 copy.48
  216.6 10.2 %all-to-all-done.1 = bf16[2,128,1536]{2,1,0:T(8,128)(2,1)S(1)} async-done(((bf16[2,128,1536]{2,1,0:T(8,128)(2,1)}), bf16[2,128,1536]{2,1,0:T(8,128)(2,1)S(1)}, u32[]{:S(2)}, u32[]{:S(2)}) %all-to-all-start.1) | async-done | bytes 786464 | tf_op jit(solution)/shard_map/all_to_all | solution.py:67
  226.8 1.3 gather_fusion.3
  228.0 0.3 gather.31
  228.4 3.9 %multiply_reduce_fusion = bf16[128,1536]{1,0:T(8,128)(2,1)} fusion(bf16[128,2,1536]{2,1,0:T(2,128)(2,1)S(1)} %gather.31, pred[128,2]{1,0:T(8,128)(4,1)S(1)} %copy.39, f32[128,2]{1,0:T(8,128)S(1)} %copy.48), kind=kLoop, calls=%fused_computation.26 | loop fusion | flops 1376256 | bytes 1180928 | tf_op jit(solution)/shard_map/reduce_sum | solution.py:74
  (25 shorter events, 0.1 us)
Async XLA Ops:
  6.5 4.7 %copy-start = (bf16[128,1536]{1,0:T(8,128)(2,1)S(1)}, bf16[128,1536]{1,0:T(8,128)(2,1)}, u32[]{:S(2)}) copy-start(bf16[128,1536]{1,0:T(8,128)(2,1)} %param.8) | copy-start | bytes 1179652
  6.5 21.8 %copy-start.2 = (s32[1,32,6]{1,0,2:T(1,128)S(1)}, s32[1,32,6]{1,0,2:T(1,128)}, u32[]{:S(2)}) copy-start(s32[1,32,6]{1,0,2:T(1,128)} %param.14) | copy-start | bytes 2308
  6.5 22.3 %copy-start.4 = (s32[1,4,48]{2,1,0:T(4,128)S(1)}, s32[1,4,48]{2,1,0:T(4,128)}, u32[]{:S(2)}) copy-start(s32[1,4,48]{2,1,0:T(4,128)} %param.15) | copy-start | bytes 2308
  6.5 85.7 %all-gather.2.cloned.1.call-start = ((), (), s32[]{:S(2)}) async-start(), calls=%async_computation.3 | async-start | bytes 3932160 | tf_op jit(solution)/shard_map/all_gather | solution.py:53
  28.1 184.5 %reduce-scatter.2.cloned.1.call-start = ((), (), s32[]{:S(2)}) async-start(), calls=%async_computation.4 | async-start | bytes 3932160 | tf_op jit(solution)/shard_map/reduce_scatter | solution.py:64
  150.5 65.8 %copy-start.3 = (s32[128,2]{0,1:T(2,128)S(1)}, s32[128,2]{0,1:T(2,128)}, u32[]{:S(2)}) copy-start(s32[128,2]{0,1:T(2,128)} %param.9) | copy-start | bytes 3076
  150.5 66.0 %copy-start.5 = (f32[128,2]{0,1:T(2,128)S(1)}, f32[128,2]{0,1:T(2,128)}, u32[]{:S(2)}) copy-start(f32[128,2]{0,1:T(2,128)} %param.10) | copy-start | bytes 3076
  153.4 78.8 %copy-start.1 = (bf16[128,1536]{1,0:T(8,128)(2,1)S(1)}, bf16[128,1536]{1,0:T(8,128)(2,1)}, u32[]{:S(2)}) copy-start(bf16[128,1536]{1,0:T(8,128)(2,1)} %param.8) | copy-start | bytes 1179652
  212.6 14.2 %all-to-all-start.1 = ((bf16[2,128,1536]{2,1,0:T(8,128)(2,1)}), bf16[2,128,1536]{2,1,0:T(8,128)(2,1)S(1)}, u32[]{:S(2)}, u32[]{:S(2)}) async-start(bf16[2,128,1536]{2,1,0:T(8,128)(2,1)} %reduce-scatter.2.cloned.1.call-done), calls=%async_computation.2 | async-start | bytes 1572864 | tf_op jit(solution)/shard_map/all_to_all | solution.py:67
Sparse Core Ops, SparseCore 0:
  28.2 63.9 all-gather.1
  153.5 59.0 reduce-scatter.1
where the time goes:
time: 239 us
  waiting for transfers between devices  132 us (55%)
  matrix products  34.5 us (14%)
  local copies, waits for them, and re-layouts  33.6 us (14%)
  blocking collectives  15.5 us (6%)
  between operations  13.6 us (6%)
  other arithmetic  5.75 us (2%)
  starting transfers between devices  3.76 us (2%)
    all_gather x1, waiting for transfers between devices, body(): arrived = lax.all_gather(incoming, 'etp', axis=2, tiled=True)  63.1 us
    reduce_scatter x1, waiting for transfers between devices, body(): lax.psum_scatter(partial_value.astype(jnp.bfloat16), 'etp', scatter_dimen...  59.2 us
    all_to_all x1, blocking collectives, body(): lax.all_to_all(outgoing, 'expert', split_axis=0, concat_axis=0, tiled=True)  15.5 us
    dot_general x1, matrix products, expert_layer(): jnp.einsum('rfki,fkio->rfo', picked, gate_part, preferred_element_type=jn...  11.8 us
    dot_general x1, matrix products, expert_layer(): jnp.einsum('rgbi,gbio->rbo', chosen, down_part, preferred_element_type=jn...  11.5 us
    dot_general x1, matrix products, expert_layer(): jnp.einsum('rfki,fkio->rfo', picked, up_part, preferred_element_type=jnp....  11.1 us
    all_to_all x1, waiting for transfers between devices, body(): lax.all_to_all(summed, 'expert', split_axis=0, concat_axis=0, tiled=True)  10.2 us
    gather x1, local copies, waits for them, and re-layouts, expert_layer(): jnp.take(hidden, sources.reshape(-1), axis=1)  8.24 us
  transfers between devices with their start and end apart: 3, of which 3 were waited for; matrix products, arithmetic and copies ran while one was open for 1% of the time, Pallas kernels for 0%

commit v1 on v0

--- a/solution.py
+++ b/solution.py
@@ -50,7 +50,16 @@
     outgoing = jnp.take(tokens, anchor, axis=0, mode="fill", fill_value=0)
     outgoing = outgoing.reshape(group_total, capacity, local_width)
     incoming = lax.all_to_all(outgoing, "expert", split_axis=0, concat_axis=0, tiled=True)
-    arrived = lax.all_gather(incoming, "etp", axis=2, tiled=True)
+    axis_total = lax.psum(1, "etp")
+    lanes = [incoming]
+    for p in range(axis_total - 1):
+        e_next = lax.ppermute(
+            lanes[-1], "etp", [(ii, (ii + 1) % axis_total) for ii in range(axis_total)]
+        )
+        lanes.append(e_next)
+    answer = jnp.concatenate(lanes[::-1], axis=2)
+    upper = lax.axis_index("etp")
+    arrived = jnp.roll(answer, shift=(upper + 1) * incoming.shape[2], axis=2)
     full_width = arrived.shape[2]
     partial_value = expert_layer(
         arrived.reshape(group_total * capacity, full_width),

time: 239 us -> 232 us (0.971)
  waiting for transfers between devices: 132 us -> 124 us
    all_gather x1 -> x0, waiting for transfers between devices: 63.1 us -> none  [body(): arrived = lax.all_gather(incoming, 'etp', axis=2, tiled=True)]
    ppermute x0 -> x3, waiting for transfers between devices: none -> 55.7 us  [body(): lax.ppermute(lanes[-1], 'etp', [(ii, (ii + 1) % axis_total) for ii in ran...]
  transfers between devices with their start and end apart: 3 -> 5, of which waited for: 3 -> 5; matrix products, arithmetic and copies ran while one was open for 1% -> 1% of each run, Pallas kernels for 0% -> 0%
where the time goes in v1:
time: 232 us
  waiting for transfers between devices  124 us (53%)
  matrix products  34.4 us (15%)
  local copies, waits for them, and re-layouts  33.8 us (15%)
  blocking collectives  14.8 us (6%)
  between operations  13.7 us (6%)
  other arithmetic  5.75 us (2%)
  starting transfers between devices  5.25 us (2%)
    reduce_scatter x1, waiting for transfers between devices, body(): lax.psum_scatter(partial_value.astype(jnp.bfloat16), 'etp', scatter_dimen...  58.2 us
    ppermute x3, waiting for transfers between devices, body(): lax.ppermute(lanes[-1], 'etp', [(ii, (ii + 1) % axis_total) for ii in ran...  55.7 us
    all_to_all x1, blocking collectives, body(): lax.all_to_all(outgoing, 'expert', split_axis=0, concat_axis=0, tiled=True)  14.8 us
    dot_general x1, matrix products, expert_layer(): jnp.einsum('rfki,fkio->rfo', picked, gate_part, preferred_element_type=jn...  11.8 us
    dot_general x1, matrix products, expert_layer(): jnp.einsum('rgbi,gbio->rbo', chosen, down_part, preferred_element_type=jn...  11.5 us
    dot_general x1, matrix products, expert_layer(): jnp.einsum('rfki,fkio->rfo', picked, up_part, preferred_element_type=jnp....  11.1 us
    all_to_all x1, waiting for transfers between devices, body(): lax.all_to_all(summed, 'expert', split_axis=0, concat_axis=0, tiled=True)  10.1 us
    gather x1, local copies, waits for them, and re-layouts, expert_layer(): jnp.take(tiles, gate_pick.reshape(-1), axis=1)  8.42 us
  transfers between devices with their start and end apart: 5, of which 5 were waited for; matrix products, arithmetic and copies ran while one was open for 1% of the time, Pallas kernels for 0%

profile of v1, /device:TPU:0, one launch (start us, length us, event | category | flops | bytes accessed | tf_op | source)
XLA Modules:
  0.0 231.8 jit_solution(1701957925171940458)
XLA Ops:
  6.5 0.8 copy.36
  7.4 0.1 eq.29
  7.5 0.1 reshape.162
  7.7 0.7 broadcast_multiply_fusion
  8.4 0.6 reduce-window.6
  9.0 0.2 slice_reduce_fusion
  9.2 0.2 reduce-window.9
  9.4 0.1 copy.42
  9.6 0.1 mul.49
  9.7 1.4 scatter_custom_fusion
  11.2 1.3 gather_fusion
  12.5 0.1 broadcast_select_fusion.6
  12.6 14.8 %all_to_all.10 = bf16[2,128,1536]{2,1,0:T(8,128)(2,1)S(1)} all-to-all(bf16[2,128,1536]{2,1,0:T(8,128)(2,1)S(1)} %broadcast_select_fusion.6), channel_id=1, replica_groups=mesh['dp'=4,'expert'=2,'etp'=4] {'expert'}, dimensions={0} | all-to-all | bytes 1572864 | tf_op jit(solution)/shard_map/all_to_all | solution.py:52
  27.4 1.7 collective-permute-start
  29.1 18.6 %collective-permute-done = bf16[2,128,1536]{2,1,0:T(8,128)(2,1)S(1)} collective-permute-done((bf16[2,128,1536]{2,1,0:T(8,128)(2,1)S(1)}, bf16[2,128,1536]{2,1,0:T(8,128)(2,1)S(1)}, u32[]{:S(2)}, u32[]{:S(2)}) %collective-permute-start) | collective-permute-done | bytes 786464 | tf_op jit(solution)/shard_map/ppermute | solution.py:56
  47.7 19.4 %collective-permute-done.1 = bf16[2,128,1536]{2,1,0:T(8,128)(2,1)S(1)} collective-permute-done((bf16[2,128,1536]{2,1,0:T(8,128)(2,1)S(1)}, bf16[2,128,1536]{2,1,0:T(8,128)(2,1)S(1)}, u32[]{:S(2)}, u32[]{:S(2)}) %collective-permute-start.1) | collective-permute-done | bytes 786464 | tf_op jit(solution)/shard_map/ppermute | solution.py:56
  67.1 0.1 copy.43
  67.4 0.1 reshape_squeeze.6
  67.5 0.1 copy.41
  67.7 0.1 copy.40
  67.9 17.8 %collective-permute-done.2 = bf16[2,128,1536]{2,1,0:T(8,128)(2,1)S(1)} collective-permute-done((bf16[2,128,1536]{2,1,0:T(8,128)(2,1)S(1)}, bf16[2,128,1536]{2,1,0:T(8,128)(2,1)S(1)}, u32[]{:S(2)}, u32[]{:S(2)}) %collective-permute-start.2) | collective-permute-done | bytes 786464 | tf_op jit(solution)/shard_map/ppermute | solution.py:56
  85.6 0.1 constant_dynamic-update-slice_fusion.7
  85.7 0.1 constant_dynamic-update-slice_fusion.6
  85.9 0.1 constant_dynamic-update-slice_fusion.5
  86.0 0.1 constant_dynamic-update-slice_fusion.4
  86.1 0.1 constant_dynamic-update-slice_fusion.3
  86.2 0.1 constant_dynamic-update-slice_fusion.2
  86.3 0.1 constant_dynamic-update-slice_fusion.1
  86.4 0.1 constant_dynamic-update-slice_fusion
  86.5 1.2 constant_dynamic-slice_fusion
  87.7 0.7 copy.54
  88.4 0.8 copy.44
  89.2 8.4 %gather_fusion.1 = bf16[192,256,128]{2,1,0:T(8,128)(2,1)} fusion(bf16[256,48,128]{2,0,1:T(8,128)(2,1)S(1)} %copy.44, s32[1024]{0:T(1024)S(1)} %get-tuple-element.6), kind=kCustom, calls=%fused_computation.1 | custom fusion | bytes 25166592 | tf_op jit(solution)/shard_map/jit(_take)/gather | solution.py:26
  97.7 11.8 %fusion.3 = f32[32,256,128,1]{2,1,3,0:T(8,128)} fusion(bf16[256,32,6,128]{3,0,2,1:T(8,128)(2,1)} %bitcast.89, pred[32,6]{1,0:T(8,128)(4,1)S(1)} %copy.41, bf16[1,32,6,128,128]{4,3,2,1,0:T(8,128)(2,1)} %param.11), kind=kOutput, calls=%fused_computation.10 | convolution fusion | flops 1616904192 | bytes 23068864 | tf_op jit(solution)/shard_map/rfki,fkio->rfo/dot_general | solution.py:29
  109.5 11.1 %fusion.10 = bf16[256,32,128]{2,0,1:T(8,128)(2,1)S(1)} fusion(f32[32,256,128,1]{2,1,3,0:T(8,128)} %fusion.3, bf16[1,32,6,128,128]{4,3,2,1,0:T(8,128)(2,1)} %param.12, bf16[256,32,6,128]{3,0,2,1:T(8,128)(2,1)} %bitcast.90, pred[32,6]{1,0:T(8,128)(4,1)S(1)} %copy.41), kind=kOutput, calls=%fused_computation.19 | convolution fusion | flops 1623195648 | bytes 25166016 | tf_op jit(solution)/shard_map/rfki,fkio->rfo/dot_general | solution.py:30
  120.6 8.2 %gather_fusion.2 = bf16[192,256,128]{2,1,0:T(8,128)(2,1)} fusion(bf16[256,32,128]{2,0,1:T(8,128)(2,1)S(1)} %fusion.10, s32[1024]{0:T(1024)S(1)} %get-tuple-element.5), kind=kCustom, calls=%fused_computation.2 | custom fusion | bytes 25166592 | tf_op jit(solution)/shard_map/jit(_take)/gather | solution.py:33
  128.8 11.5 %fusion.14 = bf16[256,48,128]{2,0,1:T(8,128)(2,1)} fusion(bf16[256,4,48,128]{3,0,2,1:T(8,128)(2,1)} %bitcast.91, pred[4,48]{0,1:T(8,128)(4,1)S(1)} %copy.40, bf16[1,4,48,128,128]{4,3,2,1,0:T(8,128)(2,1)} %param.13), kind=kOutput, calls=%fused_computation.25 | convolution fusion | flops 1618477056 | bytes 22020288 | tf_op jit(solution)/shard_map/rgbi,gbio->rbo/dot_general | solution.py:36
  140.3 3.9 %copy.47 = bf16[256,48,128]{2,1,0:T(8,128)(2,1)S(1)} copy(bf16[256,48,128]{2,0,1:T(8,128)(2,1)} %fusion.14) | data formatting | bytes 6291456 | tf_op jit(solution)/shard_map/convert_element_type | solution.py:74
  144.3 2.8 %convert_element_type.30 = bf16[2,128,6144]{2,1,0:T(8,128)(2,1)} reshape(bf16[256,48,128]{2,1,0:T(8,128)(2,1)S(1)} %copy.47) | data formatting | bytes 6291456 | tf_op jit(solution)/shard_map/convert_element_type | solution.py:74
  147.2 58.2 %reduce-scatter.2.cloned.1.call-done = bf16[2,128,1536]{2,1,0:T(8,128)(2,1)} async-done(((bf16[2,128,6144]{2,1,0:T(8,128)(2,1)}), bf16[2,128,1536]{2,1,0:T(8,128)(2,1)}) %reduce-scatter.2.cloned.1.call-update) | async-done | bytes 786448 | tf_op jit(solution)/shard_map/reduce_scatter | solution.py:73
  205.3 3.5 %all-to-all-start.1 = ((bf16[2,128,1536]{2,1,0:T(8,128)(2,1)}), bf16[2,128,1536]{2,1,0:T(8,128)(2,1)S(1)}, u32[]{:S(2)}, u32[]{:S(2)}) async-start(bf16[2,128,1536]{2,1,0:T(8,128)(2,1)} %reduce-scatter.2.cloned.1.call-done), calls=%async_computation.2 | async-start | bytes 1572864 | tf_op jit(solution)/shard_map/all_to_all | solution.py:76
  208.9 0.1 reduce_sum.23
  209.1 0.1 copy.39
  209.2 0.1 copy.48
  209.4 10.1 %all-to-all-done.1 = bf16[2,128,1536]{2,1,0:T(8,128)(2,1)S(1)} async-done(((bf16[2,128,1536]{2,1,0:T(8,128)(2,1)}), bf16[2,128,1536]{2,1,0:T(8,128)(2,1)S(1)}, u32[]{:S(2)}, u32[]{:S(2)}) %all-to-all-start.1) | async-done | bytes 786464 | tf_op jit(solution)/shard_map/all_to_all | solution.py:76
  219.5 1.3 gather_fusion.3
  220.8 0.3 gather.31
  221.1 3.9 %multiply_reduce_fusion = bf16[128,1536]{1,0:T(8,128)(2,1)} fusion(bf16[128,2,1536]{2,1,0:T(2,128)(2,1)S(1)} %gather.31, pred[128,2]{1,0:T(8,128)(4,1)S(1)} %copy.39, f32[128,2]{1,0:T(8,128)S(1)} %copy.48), kind=kLoop, calls=%fused_computation.26 | loop fusion | flops 1376256 | bytes 1180928 | tf_op jit(solution)/shard_map/reduce_sum | solution.py:83
  (36 shorter events, 0.6 us)
Async XLA Ops:
  6.5 4.7 %copy-start = (bf16[128,1536]{1,0:T(8,128)(2,1)S(1)}, bf16[128,1536]{1,0:T(8,128)(2,1)}, u32[]{:S(2)}) copy-start(bf16[128,1536]{1,0:T(8,128)(2,1)} %param.8) | copy-start | bytes 1179652
  6.5 41.2 %copy-start.2 = (s32[1,32,6]{1,0,2:T(1,128)S(1)}, s32[1,32,6]{1,0,2:T(1,128)}, u32[]{:S(2)}) copy-start(s32[1,32,6]{1,0,2:T(1,128)} %param.14) | copy-start | bytes 2308
  6.5 60.8 %copy-start.4 = (s32[1,4,48]{2,1,0:T(4,128)S(1)}, s32[1,4,48]{2,1,0:T(4,128)}, u32[]{:S(2)}) copy-start(s32[1,4,48]{2,1,0:T(4,128)} %param.15) | copy-start | bytes 2308
  6.5 198.8 %reduce-scatter.2.cloned.1.call-start = ((), (), s32[]{:S(2)}) async-start(), calls=%async_computation.3 | async-start | bytes 3932160 | tf_op jit(solution)/shard_map/reduce_scatter | solution.py:73
  27.4 20.3 %collective-permute-start = (bf16[2,128,1536]{2,1,0:T(8,128)(2,1)S(1)}, bf16[2,128,1536]{2,1,0:T(8,128)(2,1)S(1)}, u32[]{:S(2)}, u32[]{:S(2)}) collective-permute-start(bf16[2,128,1536]{2,1,0:T(8,128)(2,1)S(1)} %all_to_all.10), channel_id=1, source_target_pairs={{0,1},{1,2},{2,3},{3,0},{4,5},{5,6},{6,7},{7,4},{8,9},{9,10},{10,1... | collective-permute-start | bytes 2359304 | tf_op jit(solution)/shard_map/ppermute | solution.py:56
  47.7 19.4 %collective-permute-start.1 = (bf16[2,128,1536]{2,1,0:T(8,128)(2,1)S(1)}, bf16[2,128,1536]{2,1,0:T(8,128)(2,1)S(1)}, u32[]{:S(2)}, u32[]{:S(2)}) collective-permute-start(bf16[2,128,1536]{2,1,0:T(8,128)(2,1)S(1)} %collective-permute-done), channel_id=1, source_target_pairs={{0,1},{1,2},{2,3},{3,0},{4,5},{5,6},{6,7},{7,4},{8,9},{9,10},{10,1... | collective-permute-start | bytes 2359304 | tf_op jit(solution)/shard_map/ppermute | solution.py:56
  67.1 18.5 %collective-permute-start.2 = (bf16[2,128,1536]{2,1,0:T(8,128)(2,1)S(1)}, bf16[2,128,1536]{2,1,0:T(8,128)(2,1)S(1)}, u32[]{:S(2)}, u32[]{:S(2)}) collective-permute-start(bf16[2,128,1536]{2,1,0:T(8,128)(2,1)S(1)} %collective-permute-done.1), channel_id=1, source_target_pairs={{0,1},{1,2},{2,3},{3,0},{4,5},{5,6},{6,7},{7,4},{8,9},{9,10},{10,1... | collective-permute-start | bytes 2359304 | tf_op jit(solution)/shard_map/ppermute | solution.py:56
  144.3 64.8 %copy-start.3 = (s32[128,2]{0,1:T(2,128)S(1)}, s32[128,2]{0,1:T(2,128)}, u32[]{:S(2)}) copy-start(s32[128,2]{0,1:T(2,128)} %param.9) | copy-start | bytes 3076
  144.3 65.0 %copy-start.5 = (f32[128,2]{0,1:T(2,128)S(1)}, f32[128,2]{0,1:T(2,128)}, u32[]{:S(2)}) copy-start(f32[128,2]{0,1:T(2,128)} %param.10) | copy-start | bytes 3076
  147.1 77.8 %copy-start.1 = (bf16[128,1536]{1,0:T(8,128)(2,1)S(1)}, bf16[128,1536]{1,0:T(8,128)(2,1)}, u32[]{:S(2)}) copy-start(bf16[128,1536]{1,0:T(8,128)(2,1)} %param.8) | copy-start | bytes 1179652
  205.3 14.2 %all-to-all-start.1 = ((bf16[2,128,1536]{2,1,0:T(8,128)(2,1)}), bf16[2,128,1536]{2,1,0:T(8,128)(2,1)S(1)}, u32[]{:S(2)}, u32[]{:S(2)}) async-start(bf16[2,128,1536]{2,1,0:T(8,128)(2,1)} %reduce-scatter.2.cloned.1.call-done), calls=%async_computation.2 | async-start | bytes 1572864 | tf_op jit(solution)/shard_map/all_to_all | solution.py:76
Sparse Core Ops, SparseCore 0:
  147.3 58.0 reduce-scatter.1
